TPU v7x, 32 devices: a whole 2x2x4 slice. The times are simulated.
32 devices in a mesh: liq: 4 (over y, x), ill: 2 (over core), dur: 4 (over z).
Axes of the slice: x: 2, y: 2, z: 4, core: 2. Of those that a mesh axis runs over, the one named last changes fastest.
Arguments:
- marginal_value: float32 [32, 8, 4, 512], P(None, 'dur', 'ill', 'liq'), may hold values from 0.5 to 2
- transition: float32 [32, 32], replicated, may hold values from 0 to 1, as said below
- discount_shock: float32 [32], replicated, may hold values from 0.5 to 2
- illiquid_drift: float32 [4], P('ill'), may hold values from 0.2 to 0.8
- durable_keep: float32 [8], P('dur'), may hold values from 0.3 to 0.9
- bracket_index: int32 [32, 8, 4, 512], P(None, 'dur', 'ill', 'liq'), may hold values from 0 to 510
- bracket_weight: float32 [32, 8, 4, 512], P(None, 'dur', 'ill', 'liq'), may hold values from 0 to 1
- steady_consumption: float32 [32, 8, 4, 512], P(None, 'dur', 'ill', 'liq'), may hold values from 0.8 to 1.6
- lottery_weight: float32 [32, 8, 4, 512], P(None, 'dur', 'ill', 'liq'), may hold values from 0 to 1
- liquid_target: int32 [32, 8, 4, 512], P(None, 'dur', 'ill', 'liq'), may hold values from 0 to 510
- illiquid_target: int32 [32, 8, 4], P(None, 'dur', 'ill'), may hold values from 0 to 3
- population: float32 [32, 8, 4, 512], P(None, 'dur', 'ill', 'liq'), may hold values from 0.5 to 2
Outputs:
- consumption: float32 [32, 8, 4, 512], P(None, 'dur', 'ill', 'liq')
- population_next: float32 [32, 8, 4, 512], P(None, 'dur', 'ill', 'liq')
Inputs may be any that keep to these rules, and one draw needn't show every extreme that they name: `bracket_index`: global liquid index; the upper bracket point is index + 1. `liquid_target`: global liquid index; the upper target is index + 1. `illiquid_target`: global illiquid index. `transition`: entries positive, every row sums to one.
All inputs are finite; a program needn't handle non-finite values.
Results may differ from a plain program's by a relative error of at most 0.000065.
Values sent between devices are 32-bit elements; how exact they have to be, the bound alone decides.
A program may use at most 64 MiB of HBM per device.

v0:
```python
import jax
import jax.numpy as jnp
from jax import lax
from jax.sharding import PartitionSpec as P

DISCOUNT = 0.96
GROSS_RATE = 1.01
SLOPE_GAIN = 0.5
HIGHEST_PREC = lax.Precision.HIGHEST


def passed_along(block, axis, distance):
    devices = range(lax.axis_size(axis))
    route = [(i - distance, i) for i in devices if i - distance in devices]
    return lax.ppermute(block, axis, route)


def expect_upper(values, transition, drift_rate):
    expected = jnp.einsum("zy,ydab->zdab", transition, values, precision=HIGHEST_PREC)
    above_plane = passed_along(expected[:, :, :1, :], "ill", -1)
    is_last = lax.axis_index("ill") == lax.axis_size("ill") - 1
    above_plane = jnp.where(is_last, expected[:, :, -1:, :], above_plane)
    upper_plane = jnp.concatenate([expected[:, :, 1:, :], above_plane], axis=2)
    drift_full = drift_rate[None, None, :, None]
    return drift_full * expected + (1.0 - drift_full) * upper_plane


def backward_step(values, transition, drift_rate, shock_scale, both_index, bracket_weight):
    drifted = expect_upper(values, transition, drift_rate)
    endogenous = lax.rsqrt(DISCOUNT * GROSS_RATE * shock_scale[:, None, None, None] * drifted)
    pencil = lax.all_gather(endogenous, "liq", axis=3, tiled=True)
    liq_rows = bracket_weight.shape[3]
    picked = jnp.take_along_axis(pencil, both_index, axis=3)
    lower_value = picked[:, :, :, :liq_rows]
    upper_value = picked[:, :, :, liq_rows:]
    return bracket_weight * lower_value + (1.0 - bracket_weight) * upper_value


def scatter_pair(size, index_low, index_high, mass_low, mass_high):
    flat_index = jnp.concatenate([index_low.reshape(-1), index_high.reshape(-1)])
    flat_value = jnp.concatenate([mass_low.reshape(-1), mass_high.reshape(-1)])
    return jnp.zeros((size,), jnp.float32).at[flat_index].add(flat_value)


def joint_terms(population, share, liquid_target, illiquid_target, liq_count, ill_count):
    incomes, durables, ill_rows, liq_rows = population.shape
    inc_idx = lax.broadcasted_iota(jnp.int32, population.shape, 0)
    dur_idx = lax.broadcasted_iota(jnp.int32, population.shape, 1)
    ill_dest = jnp.broadcast_to(illiquid_target[:, :, :, None], population.shape)
    owner_ill = ill_dest // ill_rows
    local_ill = ill_dest % ill_rows

    def flat_index(target):
        owner_block = target // liq_rows * ill_count + owner_ill
        return (
            ((owner_block * incomes + inc_idx) * durables + dur_idx) * ill_rows + local_ill
        ) * liq_rows + target % liq_rows

    total = liq_count * ill_count * incomes * durables * ill_rows * liq_rows
    flat_mass = scatter_pair(
        total,
        flat_index(liquid_target),
        flat_index(liquid_target + 1),
        population * share,
        population * (1.0 - share),
    )
    return flat_mass.reshape(liq_count * ill_count * incomes, durables, ill_rows, liq_rows)


def body(
    marginal_value,
    transition,
    discount_shock,
    illiquid_drift,
    durable_keep,
    bracket_index,
    bracket_weight,
    steady_consumption,
    lottery_weight,
    liquid_target,
    illiquid_target,
    population,
):
    both_index = jnp.concatenate([bracket_index, bracket_index + 1], axis=3)
    policy_one = backward_step(
        marginal_value, transition, illiquid_drift, discount_shock, both_index, bracket_weight
    )
    value_two = GROSS_RATE / (policy_one * policy_one)
    consumption = backward_step(
        value_two,
        transition,
        illiquid_drift,
        jnp.ones_like(discount_shock),
        both_index,
        bracket_weight,
    )
    share = jnp.clip(lottery_weight + SLOPE_GAIN * (policy_one - steady_consumption), 0.0, 1.0)
    liq_count = lax.axis_size("liq")
    ill_count = lax.axis_size("ill")
    income_half = population.shape[0] // 2
    halves = []
    for half_idx in range(2):
        picked = slice(half_idx * income_half, (half_idx + 1) * income_half)
        terms = joint_terms(
            population[picked],
            share[picked],
            liquid_target[picked],
            illiquid_target[picked],
            liq_count,
            ill_count,
        )
        halves.append(lax.psum_scatter(terms, ("liq", "ill"), scatter_dimension=0, tiled=True))
    lottery_mass = jnp.concatenate(halves, axis=0)
    durables = population.shape[1]
    dur_plane = lax.axis_index("dur") * durables + lax.broadcasted_iota(jnp.int32, (durables,), 0)
    stay_share = jnp.where(dur_plane == 0, 1.0, durable_keep)[None, :, None, None]
    depart = (1.0 - stay_share) * lottery_mass
    incoming = passed_along(depart[:, :1], "dur", -1)
    settled = stay_share * lottery_mass + jnp.concatenate([depart[:, 1:], incoming], axis=1)
    population_next = jnp.einsum("zy,zdab->ydab", transition, settled, precision=HIGHEST_PREC)
    return (consumption, population_next)


def solution(mesh):
    in_specs = (
        P(None, "dur", "ill", "liq"),
        P(),
        P(),
        P("ill"),
        P("dur"),
        P(None, "dur", "ill", "liq"),
        P(None, "dur", "ill", "liq"),
        P(None, "dur", "ill", "liq"),
        P(None, "dur", "ill", "liq"),
        P(None, "dur", "ill", "liq"),
        P(None, "dur", "ill"),
        P(None, "dur", "ill", "liq"),
    )
    out_specs = (P(None, "dur", "ill", "liq"), P(None, "dur", "ill", "liq"))
    return jax.shard_map(body, mesh=mesh, in_specs=in_specs, out_specs=out_specs, check_vma=False)
```

profile of v0, /device:TPU:0, one launch (start us, length us, event | category | flops | bytes accessed | tf_op | source)
XLA Modules:
  0.0 965.2 jit_solution(3605320922015979585)
XLA Ops:
  7.3 0.7 copy-done
  8.0 0.9 fusion.15
  8.9 1.3 collective-permute-start
  10.2 0.8 broadcast_add_fusion.3
  11.2 0.8 compare_and_fusion.2
  13.2 0.8 fusion.39
  14.5 0.4 copy-done.11
  14.8 0.6 dynamic-slice
  16.2 12.9 %all_gather.6 = f32[32,2,2,512]{3,0,2,1:T(8,128)S(1)} all-gather(f32[32,2,2,128]{3,0,2,1:T(8,128)S(1)} %fusion.8), channel_id=1, replica_groups=mesh['liq'=4,'ill'=2,'dur'=4] {'liq'}, dimensions={3}, use_global_device_ids=true | all-gather | bytes 327680 | tf_op jit(solution)/shard_map/all_gather | solution.py:31
  29.1 366.2 %gather_fusion = f32[32768]{0:T(1024)S(1)} fusion(f32[32,2,2,512]{3,0,2,1:T(8,128)S(1)} %all_gather.6, s32[32768]{0:T(1024)S(1)} %bitcast.33), kind=kCustom, calls=%fused_computation.clone | custom fusion | bytes 786432 | tf_op jit(solution)/shard_map/jit(take_along_axis)/gather | solution.py:33
  395.6 0.6 copy-done.2
  396.5 0.5 copy-done.3
  397.0 0.2 convolution_bitcast_fusion.1
  397.2 1.3 collective-permute-start.1
  398.7 86.5 %scatter_custom_fusion = f32[65536]{0:T(1024)} fusion(s32[16384]{0:T(1024)S(1)} %bitcast.46, f32[16384]{0:T(1024)S(1)} %pad_maximum_fusion, f32[]{:T(128)} %constant.136.clone.1), kind=kCustom, calls=%fused_computation.13 | custom fusion | flops 16384 | bytes 262148 | tf_op jit(solution)/shard_map/scatter-add | solution.py:42
  485.2 86.5 %scatter_custom_fusion.1 = f32[65536]{0:T(1024)} fusion(s32[16384]{0:T(1024)S(1)} %bitcast.47, f32[16384]{0:T(1024)S(1)} %pad_maximum_fusion.1, f32[]{:T(128)} %constant.136.clone.1), kind=kCustom, calls=%fused_computation.11 | custom fusion | flops 16384 | bytes 262148 | tf_op jit(solution)/shard_map/scatter-add | solution.py:42
  571.8 12.4 %all_gather.7 = f32[32,2,2,512]{3,0,2,1:T(8,128)S(1)} all-gather(f32[32,2,2,128]{3,0,2,1:T(8,128)S(1)} %fusion.11), channel_id=1, replica_groups=mesh['liq'=4,'ill'=2,'dur'=4] {'liq'}, dimensions={3}, use_global_device_ids=true | all-gather | bytes 327680 | tf_op jit(solution)/shard_map/all_gather | solution.py:31
  584.2 366.2 %gather_fusion.1 = f32[32768]{0:T(1024)S(1)} fusion(f32[32,2,2,512]{3,0,2,1:T(8,128)S(1)} %all_gather.7, s32[32768]{0:T(1024)S(1)} %bitcast.34), kind=kCustom, calls=%fused_computation.1.clone | custom fusion | bytes 786432 | tf_op jit(solution)/shard_map/jit(take_along_axis)/gather | solution.py:33
  950.7 0.8 constant_dynamic-slice_fusion
  951.6 1.3 collective-permute-start.2
  952.9 0.7 fusion.4
  953.6 3.8 collective-permute-done.2
  957.4 0.3 convolution_bitcast_fusion
  957.7 0.7 copy.81
  (64 shorter events, 2.8 us)
Async XLA Ops:
  7.2 0.8 copy-start
  7.2 4.9 copy-start.8
  7.2 4.9 copy-start.10
  7.2 4.9 copy-start.1
  7.2 6.0 copy-start.6
  7.2 943.4 %all-reduce.5.cloned.1.call-start = ((), (), s32[]{:S(2)}) async-start(), calls=%async_computation | async-start | bytes 1048576
  8.9 7.1 collective-permute-start
  13.2 1.0 copy-start.9
  14.2 0.7 copy-start.11
  395.4 0.8 copy-start.2
  395.4 0.9 copy-start.4
  395.4 0.9 copy-start.5
  396.3 0.7 copy-start.3
  396.4 2.1 copy-start.7
  397.2 174.4 %collective-permute-start.1 = (f32[32,2,1,128]{3,0,2,1:T(8,128)S(1)}, f32[32,2,1,128]{3,0,2,1:T(8,128)S(1)}, u32[]{:S(2)}, u32[]{:S(2)}) collective-permute-start(f32[32,2,1,128]{3,0,2,1:T(8,128)S(1)} %slice.87), channel_id=1, source_target_pairs={{4,0},{5,1},{6,2},{7,3},{12,8},{13,9},{14,10},{15,11},{20,16},{21,... | collective-permute-start | bytes 98312 | tf_op jit(solution)/shard_map/ppermute | solution.py:15
  951.6 5.8 collective-permute-start.2
Sparse Core Ops, SparseCore 0:
  571.8 55.9 all-reduce.4
where the time goes:
time: 966 us; the launch traced here: 965 us
  local copies, waits for them, and re-layouts  738 us (76%)
  other arithmetic  177 us (18%)
  blocking collectives  25.3 us (3%)
  between operations  15.1 us (2%)
    gather x4, local copies, waits for them, and re-layouts, backward_step(): picked = jnp.take_along_axis(pencil, both_index, axis=3)  733 us
    scatter-add x2, other arithmetic, scatter_pair(): return jnp.zeros((size,), jnp.float32).at[flat_index].add(flat_value)  173 us
    all_gather x2, blocking collectives, backward_step(): pencil = lax.all_gather(endogenous, 'liq', axis=3, tiled=True)  25.3 us
  transfers between devices with their start and end apart: 4, of which 1 were waited for; matrix products, arithmetic and copies ran while one was open for 56% of the time, Pallas kernels for 0%

commit v1 on v0

v1 whole, which is shorter than its diff:
```python
import functools

import jax
import jax.numpy as jnp
from jax import lax
from jax.experimental import pallas as pl
from jax.experimental.pallas import tpu as pltpu
from jax.sharding import PartitionSpec as P

DISCOUNT = 0.96
GROSS_RATE = 1.01
SLOPE_GAIN = 0.5
HIGHEST_PREC = lax.Precision.HIGHEST
MESH_ID = pl.DeviceIdType.MESH
NT = (((1,), (1,)), ((), ()))
TILE = 8


def split_by(x, n):
    if n & (n - 1) == 0:
        return x >> (n.bit_length() - 1), x & (n - 1)
    return lax.div(x, jnp.int32(n)), lax.rem(x, jnp.int32(n))


def dot(a, b):
    return jnp.dot(a, b, precision=HIGHEST_PREC, preferred_element_type=jnp.float32)


def iota(shape, axis):
    return lax.broadcasted_iota(jnp.int32, shape, axis)


def as_float(flag):
    return jnp.where(flag, jnp.float32(1.0), jnp.float32(0.0))


def kernel(
    dims,
    value_ref, transition_ref, shock_ref, drift_ref, keep_ref, index_ref, weight_ref,
    steady_ref, lottery_ref, target_ref, ill_target_ref, population_ref,
    consumption_ref, next_ref,
    first_mat, first_up, second_mat, second_up, next_mat, next_in,
    near_value, value_two, pencil, policy, mass_low, mass_high, target_hi, target_lo,
    terms, terms_in, owner_sum, owner_in, settled, depart, depart_in,
    value_send, value_recv, pencil_send, pencil_recv, terms_send, terms_recv,
    owner_send, owner_recv, depart_send, depart_recv,
):
    incomes, durables, ill_rows, liq_rows, liq_n, ill_n, dur_n = dims
    group = durables * ill_rows
    rows = incomes * group
    plane_rows = incomes * ill_rows
    liq_me, ill_me, dur_me = (lax.axis_index(name) for name in ("liq", "ill", "dur"))

    barrier = pltpu.get_barrier_semaphore()
    for step in range(1, liq_n):
        pl.semaphore_signal(barrier, inc=1, device_id={"liq": lax.rem(liq_me + step, liq_n)}, device_id_type=MESH_ID)
    for step in range(1, ill_n):
        pl.semaphore_signal(barrier, inc=1, device_id={"ill": lax.rem(ill_me + step, ill_n)}, device_id_type=MESH_ID)

    @pl.when(dur_me > 0)
    def _():
        pl.semaphore_signal(barrier, inc=1, device_id={"dur": dur_me - 1}, device_id_type=MESH_ID)

    @pl.when(dur_me < dur_n - 1)
    def _():
        pl.semaphore_signal(barrier, inc=1, device_id={"dur": dur_me + 1}, device_id_type=MESH_ID)

    dur_peers = jnp.minimum(dur_me, 1) + jnp.minimum(dur_n - 1 - dur_me, 1)
    pl.semaphore_wait(barrier, liq_n - 1 + ill_n - 1 + dur_peers)

    ill_below = lax.rem(ill_me + ill_n - 1, ill_n)

    def value_copy(k, source):
        return pltpu.make_async_remote_copy(
            src_ref=source, dst_ref=near_value.at[k], send_sem=value_send.at[k],
            recv_sem=value_recv.at[k], device_id={"ill": ill_below}, device_id_type=MESH_ID,
        )

    def pencil_copy(k, step):
        peer = lax.rem(liq_me + step, liq_n)
        return pltpu.make_async_remote_copy(
            src_ref=pencil.at[k * liq_n + liq_me], dst_ref=pencil.at[k * liq_n + liq_me],
            send_sem=pencil_send.at[k * liq_n + step], recv_sem=pencil_recv.at[k * liq_n + step],
            device_id={"liq": peer}, device_id_type=MESH_ID,
        )

    def terms_copy(step):
        peer = lax.rem(ill_me + step, ill_n)
        return pltpu.make_async_remote_copy(
            src_ref=terms.at[pl.ds(peer * (liq_n * rows), liq_n * rows)], dst_ref=terms_in.at[step - 1],
            send_sem=terms_send.at[step - 1], recv_sem=terms_recv.at[step - 1],
            device_id={"ill": peer}, device_id_type=MESH_ID,
        )

    def owner_copy(step):
        peer = lax.rem(liq_me + step, liq_n)
        return pltpu.make_async_remote_copy(
            src_ref=owner_sum.at[peer], dst_ref=owner_in.at[step - 1],
            send_sem=owner_send.at[step - 1], recv_sem=owner_recv.at[step - 1],
            device_id={"liq": peer}, device_id_type=MESH_ID,
        )

    value_copy(0, value_ref).start()

    transition = transition_ref[...]
    row_z, row_rest = split_by(iota((rows, rows), 0), group)
    col_z, col_rest = split_by(iota((rows, rows), 1), group)
    row_d, row_a = split_by(row_rest, ill_rows)
    col_d, col_a = split_by(col_rest, ill_rows)
    spread = as_float(split_by(iota((rows, incomes), 0), group)[0] == iota((rows, incomes), 1))
    spread_t = as_float(iota((incomes, rows), 0) == split_by(iota((incomes, rows), 1), group)[0])
    drift = jnp.zeros((rows, rows), jnp.float32)
    for a in range(ill_rows):
        drift = jnp.where(row_a == a, drift_ref[a], drift)
    is_last = as_float(ill_me == ill_n - 1)
    same_d = row_d == col_d
    top_row = row_a == ill_rows - 1
    local = jnp.where(col_a == row_a, drift, 0.0)
    local = local + jnp.where(col_a == row_a + 1, 1.0 - drift, 0.0)
    local = local + jnp.where(top_row & (col_a == ill_rows - 1), is_last * (1.0 - drift), 0.0)
    local = jnp.where(same_d, local, 0.0)
    upper = jnp.where(same_d & top_row & (col_a == 0), (1.0 - is_last) * (1.0 - drift), 0.0)
    constant = jnp.float32(DISCOUNT * GROSS_RATE)
    eye = iota((incomes, incomes), 0) == iota((incomes, incomes), 1)
    scaled = dot(jnp.where(eye, constant * shock_ref[...], 0.0), transition)
    wide = dot(dot(spread, scaled), spread_t)
    first_mat[...] = wide * local
    first_up[...] = wide * upper

    value_copy(0, value_ref).wait_recv()
    drifted = dot(first_mat[...], value_ref[...]) + dot(first_up[...], near_value[0])
    pencil[liq_me] = lax.rsqrt(drifted)
    for step in range(1, liq_n):
        pencil_copy(0, step).start()

    wide = constant * dot(dot(spread, transition), spread_t)
    second_mat[...] = wide * local
    second_up[...] = wide * upper

    first_d = as_float(dur_me == 0)
    stay = [keep_ref[d] for d in range(durables)]
    stay[0] = first_d + (1.0 - first_d) * stay[0]
    back_d, back_rest = split_by(iota((rows, rows), 1), plane_rows)
    back_a = split_by(back_rest, ill_rows)[1]
    stays = jnp.zeros((rows, rows), jnp.float32)
    for d in range(durables):
        stays = jnp.where(back_d == d, stay[d], stays)
    mix = jnp.where(back_d == row_d, stays, 0.0) + jnp.where(back_d == row_d + 1, 1.0 - stays, 0.0)
    mix = jnp.where(back_a == row_a, mix, 0.0)
    back_z = split_by(split_by(iota((incomes, rows), 1), plane_rows)[1], ill_rows)[0]
    turned = lax.dot_general(spread, transition, NT, precision=HIGHEST_PREC, preferred_element_type=jnp.float32)
    wide = dot(turned, as_float(iota((incomes, rows), 0) == back_z))
    next_mat[...] = wide * mix
    in_z, in_a = split_by(iota((incomes, plane_rows), 1), ill_rows)
    wide = dot(turned, as_float(iota((incomes, plane_rows), 0) == in_z))
    in_row = split_by(iota((rows, plane_rows), 0), group)[1]
    in_row_d, in_row_a = split_by(in_row, ill_rows)
    in_col_a = split_by(iota((rows, plane_rows), 1), ill_rows)[1]
    next_in[...] = jnp.where((in_row_d == durables - 1) & (in_row_a == in_col_a), wide, 0.0)

    def block_of(position):
        block = jnp.zeros(position.shape, jnp.int32)
        for h in range(1, liq_n):
            block = block + jnp.where(position >= h * liq_rows, 1, 0)
        return block, position - block * liq_rows

    target = target_ref[...]
    target_hi[...], target_lo[...] = block_of(target)

    def interpolate(k, tile):
        span = pl.ds(tile * TILE, TILE)
        index = index_ref[span, :]
        low_block, low_lane = block_of(index)
        high_block, high_lane = block_of(index + 1)
        low = high = None
        for h in range(liq_n):
            block = pencil[k * liq_n + h, span, :]
            low_h = jnp.take_along_axis(block, low_lane, axis=1, mode="promise_in_bounds")
            high_h = jnp.take_along_axis(block, high_lane, axis=1, mode="promise_in_bounds")
            low = low_h if h == 0 else jnp.where(low_block == h, low_h, low)
            high = high_h if h == 0 else jnp.where(high_block == h, high_h, high)
        weight = weight_ref[span, :]
        return weight * low + (1.0 - weight) * high

    for step in range(1, liq_n):
        pencil_copy(0, step).wait_recv()
    for tile in range(rows // TILE):
        span = pl.ds(tile * TILE, TILE)
        chosen = interpolate(0, tile)
        policy[span, :] = chosen
        value_two[span, :] = GROSS_RATE / (chosen * chosen)
    value_copy(1, value_two).start()

    share = jnp.clip(lottery_ref[...] + SLOPE_GAIN * (policy[...] - steady_ref[...]), 0.0, 1.0)
    mass = population_ref[...]
    mass_low[...] = mass * share
    mass_high[...] = mass * (1.0 - share)

    lanes = 2 * liq_n
    sub = iota((lanes, liq_rows), 0)
    lane = iota((lanes, liq_rows), 1)
    sub_block = jnp.where(sub < liq_n, sub, sub - liq_n)
    lane_row = iota((liq_rows, liq_rows), 0)
    per_tile = TILE // group

    def scatter_tile(tile, carry):
        span = pl.ds(pl.multiple_of(tile * TILE, TILE), TILE)
        low_t, high_t, hi_t, lo_t = mass_low[span, :], mass_high[span, :], target_hi[span, :], target_lo[span, :]
        for zz in range(per_tile):
            z = tile * per_tile + zz
            for d in range(durables):
                totals = []
                for a in range(ill_rows):
                    k = zz * group + d * ill_rows + a
                    both = jnp.where(sub < liq_n, low_t[k : k + 1, :], high_t[k : k + 1, :])
                    both = jnp.where(hi_t[k : k + 1, :] == sub_block, both, 0.0)
                    rounded = both.astype(jnp.bfloat16).astype(jnp.float32)
                    parts = jnp.concatenate([both, both - rounded], axis=0).astype(jnp.bfloat16)
                    hot = as_float(lane_row == lo_t[k : k + 1, :]).astype(jnp.bfloat16)
                    placed = lax.dot_general(parts, hot, NT, preferred_element_type=jnp.float32)
                    placed = placed[:lanes] + placed[lanes:]
                    moved = pltpu.roll(placed, 1, 1)
                    same = pltpu.roll(moved, liq_n, 0)
                    prior = pltpu.roll(moved, liq_n + 1, 0)
                    totals.append(placed + jnp.where(lane > 0, same, jnp.where(sub > 0, prior, 0.0)))
                for dest in range(ill_n * ill_rows):
                    out = None
                    for a in range(ill_rows):
                        here = as_float(ill_target_ref[d * ill_rows + a, z] == dest) * totals[a]
                        out = here if out is None else out + here
                    base = (dest // ill_rows) * liq_n * rows + d * plane_rows + z * ill_rows + dest % ill_rows
                    terms[pl.ds(base, liq_n, stride=rows), :] = out[:liq_n]
        return carry

    tiles = rows // TILE
    lax.fori_loop(0, tiles // 2, scatter_tile, 0)

    value_copy(1, value_two).wait_recv()
    drifted = dot(second_mat[...], value_two[...]) + dot(second_up[...], near_value[1])
    pencil[liq_n + liq_me] = lax.rsqrt(drifted)
    for step in range(1, liq_n):
        pencil_copy(1, step).start()

    lax.fori_loop(tiles // 2, tiles, scatter_tile, 0)
    for step in range(1, ill_n):
        terms_copy(step).start()
    for step in range(1, ill_n):
        terms_copy(step).wait_recv()
    for h in range(liq_n):
        total = terms[pl.ds(pl.multiple_of((ill_me * liq_n + h) * rows, TILE), rows), :]
        for step in range(1, ill_n):
            total = total + terms_in[step - 1, pl.ds(h * rows, rows), :]
        owner_sum[h] = total
    for step in range(1, liq_n):
        owner_copy(step).start()

    for step in range(1, liq_n):
        pencil_copy(1, step).wait_recv()
    for tile in range(rows // TILE):
        consumption_ref[pl.ds(tile * TILE, TILE), :] = interpolate(1, tile)

    for step in range(1, liq_n):
        owner_copy(step).wait_recv()
    total = owner_sum[liq_me]
    for step in range(1, liq_n):
        total = total + owner_in[step - 1]
    settled[...] = total
    depart[...] = (1.0 - stay[0]) * total[:plane_rows]

    depart_copy = pltpu.make_async_remote_copy(
        src_ref=depart, dst_ref=depart_in, send_sem=depart_send.at[0], recv_sem=depart_recv.at[0],
        device_id={"dur": jnp.maximum(dur_me - 1, 0)}, device_id_type=MESH_ID,
    )

    @pl.when(dur_me > 0)
    def _():
        depart_copy.start()

    next_ref[...] = dot(next_mat[...], settled[...])

    @pl.when(dur_me < dur_n - 1)
    def _():
        depart_copy.wait_recv()
        next_ref[...] += dot(next_in[...], depart_in[...])

    value_copy(0, value_ref).wait_send()
    value_copy(1, value_two).wait_send()
    for step in range(1, liq_n):
        pencil_copy(0, step).wait_send()
        pencil_copy(1, step).wait_send()
        owner_copy(step).wait_send()
    for step in range(1, ill_n):
        terms_copy(step).wait_send()

    @pl.when(dur_me > 0)
    def _():
        depart_copy.wait_send()


def body(
    marginal_value,
    transition,
    discount_shock,
    illiquid_drift,
    durable_keep,
    bracket_index,
    bracket_weight,
    steady_consumption,
    lottery_weight,
    liquid_target,
    illiquid_target,
    population,
):
    shape = marginal_value.shape
    incomes, durables, ill_rows, liq_rows = shape
    liq_n, ill_n, dur_n = (lax.axis_size(name) for name in ("liq", "ill", "dur"))
    rows = incomes * durables * ill_rows
    plane_rows = incomes * ill_rows
    flat = lambda x: x.reshape(rows, liq_rows)
    vmem = pl.BlockSpec(memory_space=pltpu.VMEM)
    smem = pl.BlockSpec(memory_space=pltpu.SMEM)
    f32 = jnp.float32
    block = (rows, liq_rows)
    dma = pltpu.SemaphoreType.DMA
    result = jax.ShapeDtypeStruct(block, f32)
    dims = (incomes, durables, ill_rows, liq_rows, liq_n, ill_n, dur_n)
    outs = pl.pallas_call(
        functools.partial(kernel, dims),
        out_shape=(result, result),
        in_specs=[vmem, vmem, vmem, smem, smem, vmem, vmem, vmem, vmem, vmem, smem, vmem],
        out_specs=(vmem, vmem),
        scratch_shapes=[
            pltpu.VMEM((rows, rows), f32),
            pltpu.VMEM((rows, rows), f32),
            pltpu.VMEM((rows, rows), f32),
            pltpu.VMEM((rows, rows), f32),
            pltpu.VMEM((rows, rows), f32),
            pltpu.VMEM((rows, plane_rows), f32),
            pltpu.VMEM((2,) + block, f32),
            pltpu.VMEM(block, f32),
            pltpu.VMEM((2 * liq_n,) + block, f32),
            pltpu.VMEM(block, f32),
            pltpu.VMEM(block, f32),
            pltpu.VMEM(block, f32),
            pltpu.VMEM(block, jnp.int32),
            pltpu.VMEM(block, jnp.int32),
            pltpu.VMEM((ill_n * liq_n * rows, liq_rows), f32),
            pltpu.VMEM((ill_n - 1, liq_n * rows, liq_rows), f32),
            pltpu.VMEM((liq_n,) + block, f32),
            pltpu.VMEM((liq_n - 1,) + block, f32),
            pltpu.VMEM(block, f32),
            pltpu.VMEM((plane_rows, liq_rows), f32),
            pltpu.VMEM((plane_rows, liq_rows), f32),
            dma((2,)),
            dma((2,)),
            dma((2 * liq_n,)),
            dma((2 * liq_n,)),
            dma((ill_n - 1,)),
            dma((ill_n - 1,)),
            dma((liq_n - 1,)),
            dma((liq_n - 1,)),
            dma((1,)),
            dma((1,)),
        ],
        compiler_params=pltpu.CompilerParams(collective_id=0, has_side_effects=True),
        name="window",
    )(
        flat(marginal_value),
        transition,
        discount_shock.reshape(1, incomes),
        illiquid_drift,
        durable_keep,
        flat(bracket_index),
        flat(bracket_weight),
        flat(steady_consumption),
        flat(lottery_weight),
        flat(liquid_target),
        jnp.transpose(illiquid_target, (1, 2, 0)).reshape(durables * ill_rows, incomes),
        flat(population),
    )
    return tuple(out.reshape(shape) for out in outs)


def solution(mesh):
    in_specs = (
        P(None, "dur", "ill", "liq"),
        P(),
        P(),
        P("ill"),
        P("dur"),
        P(None, "dur", "ill", "liq"),
        P(None, "dur", "ill", "liq"),
        P(None, "dur", "ill", "liq"),
        P(None, "dur", "ill", "liq"),
        P(None, "dur", "ill", "liq"),
        P(None, "dur", "ill"),
        P(None, "dur", "ill", "liq"),
    )
    out_specs = (P(None, "dur", "ill", "liq"), P(None, "dur", "ill", "liq"))
    return jax.shard_map(body, mesh=mesh, in_specs=in_specs, out_specs=out_specs, check_vma=False)
```

time: 966 us -> 31.3 us (0.03)
  local copies, waits for them, and re-layouts: 738 us -> 2.14 us
  other arithmetic: 177 us -> 0 us
  Pallas kernels: 0 us -> 28.3 us
  blocking collectives: 25.3 us -> 0 us
  between operations: 15.1 us -> 0.65 us
    gather x4 -> x0, local copies, waits for them, and re-layouts: 733 us -> none  [backward_step(): picked = jnp.take_along_axis(pencil, both_index, axis=3)]
    scatter-add x2 -> x0, other arithmetic: 173 us -> none  [scatter_pair(): return jnp.zeros((size,), jnp.float32).at[flat_index].add(flat_value)]
    pallas_call x0 -> x1, Pallas kernels: none -> 28.3 us  [body(): pl.pallas_call(functools.partial(kernel, dims), out_shape=(result, result...]
    all_gather x2 -> x0, blocking collectives: 25.3 us -> none  [backward_step(): pencil = lax.all_gather(endogenous, 'liq', axis=3, tiled=True)]
  transfers between devices with their start and end apart: 4 -> 0, of which waited for: 1 -> 0; matrix products, arithmetic and copies ran while one was open for 56% -> 0% of each run, Pallas kernels for 0% -> 0%
where the time goes in v1:
time: 31.3 us; the launch traced here: 31.1 us
  Pallas kernels  28.3 us (90%)
  local copies, waits for them, and re-layouts  2.14 us (7%)
  between operations  0.65 us (2%)
    pallas_call x1, Pallas kernels, body(): pl.pallas_call(functools.partial(kernel, dims), out_shape=(result, result...  28.3 us
    unnamed x4, local copies, waits for them, and re-layouts  2.14 us

profile of v1, /device:TPU:0, one launch (start us, length us, event | category | flops | bytes accessed | tf_op | source)
XLA Modules:
  0.0 31.1 jit_solution(2436807493579280289)
XLA Ops:
  0.6 28.3 %window.1 = (f32[128,128]{1,0:T(8,128)}, f32[128,128]{1,0:T(8,128)}) custom-call(f32[128,128]{1,0:T(8,128)} %bitcast.15, f32[32,32]{1,0:T(8,128)} %transition_ref.1, f32[1,32]{1,0:T(1,128)} %bitcast.23, f32[2]{0:T(128)} %drift_ref.1, f32[2]{0:T(128)} %keep_ref.1, s32[128,128]{1,0:T(8,128)} %bitcast.16, f32[128,128]{1,0:T(8,128)} %bitcast.17, ...), custom_call_target="tpu_custom_call" | custom-call | tf_op jit(solution)/shard_map/window/pallas_call | solution.py:327
  28.9 0.0 copy-start
  28.9 1.5 %copy.16 = f32[32,2,2,128]{3,2,1,0:T(2,128)} copy(f32[32,2,2,128]{3,2,1,0:T(2,128)} %bitcast.14) | data formatting | bytes 131072
  30.5 0.0 copy-done
  30.5 0.6 %copy.17 = f32[32,2,2,128]{3,2,1,0:T(2,128)} copy(f32[32,2,2,128]{3,2,1,0:T(2,128)S(1)} %bitcast.13) | data formatting | bytes 131072
Async XLA Ops:
  28.9 1.5 %copy-start = (f32[128,128]{1,0:T(8,128)S(1)}, f32[128,128]{1,0:T(8,128)}, u32[]{:S(2)}) copy-start(f32[128,128]{1,0:T(8,128)} %get-tuple-element.5) | copy-start | bytes 196612

commit v2 on v1

v2 whole, which is shorter than its diff:
```python
import functools

import jax
import jax.numpy as jnp
from jax import lax
from jax.experimental import pallas as pl
from jax.experimental.pallas import tpu as pltpu
from jax.sharding import PartitionSpec as P

DISCOUNT = 0.96
GROSS_RATE = 1.01
SLOPE_GAIN = 0.5
HIGHEST_PREC = lax.Precision.HIGHEST
MESH_ID = pl.DeviceIdType.MESH
NT = (((1,), (1,)), ((), ()))
TILE = 8


def split_by(x, n):
    if n & (n - 1) == 0:
        return x >> (n.bit_length() - 1), x & (n - 1)
    return lax.div(x, jnp.int32(n)), lax.rem(x, jnp.int32(n))


def dot(a, b):
    return jnp.dot(a, b, precision=HIGHEST_PREC, preferred_element_type=jnp.float32)


def iota(shape, axis):
    return lax.broadcasted_iota(jnp.int32, shape, axis)


def as_float(flag):
    return jnp.where(flag, jnp.float32(1.0), jnp.float32(0.0))


def peer_of(me, step, n):
    if n & (n - 1):
        return lax.rem(me + step, n)
    out = me
    for bit in range(n.bit_length() - 1):
        if step >> bit & 1:
            out = out + (1 - 2 * lax.rem(lax.div(me, jnp.int32(1 << bit)), jnp.int32(2))) * (1 << bit)
    return out


def kernel(
    dims,
    value_hbm, transition_hbm, shock_hbm, drift_ref, keep_ref, index_hbm, weight_hbm,
    steady_hbm, lottery_hbm, target_hbm, ill_target_ref, population_hbm,
    consumption_hbm, next_hbm,
    value_ref, transition_ref, shock_ref, index_ref, weight_ref, steady_ref, lottery_ref, target_ref,
    population_ref, consumption_ref, next_ref, load_sem, store_sem,
    first_mat, first_up, second_mat, second_up, next_mat, next_in,
    near_value, value_two, pencil, mass_low, mass_high, target_hi, target_lo,
    terms, terms_in, owner_sum, owner_in, settled, depart, depart_in,
    value_send, value_recv, pencil_send, pencil_recv, terms_send, terms_recv,
    owner_send, owner_recv, depart_send, depart_recv,
):
    incomes, durables, ill_rows, liq_rows, liq_n, ill_n, dur_n = dims
    group = durables * ill_rows
    rows = incomes * group
    half_rows = rows // 2
    plane_rows = incomes * ill_rows
    liq_me, ill_me, dur_me = (lax.axis_index(name) for name in ("liq", "ill", "dur"))
    far_first = range(liq_n - 1, 0, -1)

    barrier = pltpu.get_barrier_semaphore()
    for step in far_first:
        pl.semaphore_signal(barrier, inc=1, device_id={"liq": peer_of(liq_me, step, liq_n)}, device_id_type=MESH_ID)
    for step in range(1, ill_n):
        pl.semaphore_signal(barrier, inc=1, device_id={"ill": peer_of(ill_me, step, ill_n)}, device_id_type=MESH_ID)

    @pl.when(dur_me > 0)
    def _():
        pl.semaphore_signal(barrier, inc=1, device_id={"dur": dur_me - 1}, device_id_type=MESH_ID)

    @pl.when(dur_me < dur_n - 1)
    def _():
        pl.semaphore_signal(barrier, inc=1, device_id={"dur": dur_me + 1}, device_id_type=MESH_ID)

    loads = [
        pltpu.make_async_copy(source, held, load_sem.at[slot])
        for slot, (source, held) in enumerate((
            (transition_hbm, transition_ref), (shock_hbm, shock_ref), (value_hbm, value_ref),
            (index_hbm, index_ref), (weight_hbm, weight_ref), (target_hbm, target_ref),
            (lottery_hbm, lottery_ref), (steady_hbm, steady_ref), (population_hbm, population_ref),
        ))
    ]
    for load in loads:
        load.start()
    loads[0].wait()
    loads[1].wait()

    transition = transition_ref[...]
    row_z, row_rest = split_by(iota((rows, rows), 0), group)
    col_z, col_rest = split_by(iota((rows, rows), 1), group)
    row_d, row_a = split_by(row_rest, ill_rows)
    col_d, col_a = split_by(col_rest, ill_rows)
    spread = as_float(split_by(iota((rows, incomes), 0), group)[0] == iota((rows, incomes), 1))
    spread_t = as_float(iota((incomes, rows), 0) == split_by(iota((incomes, rows), 1), group)[0])
    drift = jnp.zeros((rows, rows), jnp.float32)
    for a in range(ill_rows):
        drift = jnp.where(row_a == a, drift_ref[a], drift)
    is_last = as_float(ill_me == ill_n - 1)
    same_d = row_d == col_d
    top_row = row_a == ill_rows - 1
    local = jnp.where(col_a == row_a, drift, 0.0)
    local = local + jnp.where(col_a == row_a + 1, 1.0 - drift, 0.0)
    local = local + jnp.where(top_row & (col_a == ill_rows - 1), is_last * (1.0 - drift), 0.0)
    local = jnp.where(same_d, local, 0.0)
    upper = jnp.where(same_d & top_row & (col_a == 0), (1.0 - is_last) * (1.0 - drift), 0.0)
    constant = jnp.float32(DISCOUNT * GROSS_RATE)
    eye = iota((incomes, incomes), 0) == iota((incomes, incomes), 1)
    scaled = dot(jnp.where(eye, constant * shock_ref[...], 0.0), transition)
    wide = dot(dot(spread, scaled), spread_t)
    first_mat[...] = wide * local
    first_up[...] = wide * upper

    dur_peers = jnp.minimum(dur_me, 1) + jnp.minimum(dur_n - 1 - dur_me, 1)
    pl.semaphore_wait(barrier, liq_n - 1 + ill_n - 1 + dur_peers)

    ill_below = lax.rem(ill_me + ill_n - 1, ill_n)

    def value_copy(k, source):
        return pltpu.make_async_remote_copy(
            src_ref=source, dst_ref=near_value.at[k], send_sem=value_send.at[k],
            recv_sem=value_recv.at[k], device_id={"ill": ill_below}, device_id_type=MESH_ID,
        )

    def pencil_copy(k, half, step):
        slot = (k * 2 + half) * liq_n + step
        part = pencil.at[k * liq_n + liq_me, pl.ds(half * half_rows, half_rows)]
        return pltpu.make_async_remote_copy(
            src_ref=part, dst_ref=part, send_sem=pencil_send.at[slot], recv_sem=pencil_recv.at[slot],
            device_id={"liq": peer_of(liq_me, step, liq_n)}, device_id_type=MESH_ID,
        )

    def terms_copy(d, step):
        peer = peer_of(ill_me, step, ill_n)
        slot = d * (ill_n - 1) + step - 1
        return pltpu.make_async_remote_copy(
            src_ref=terms.at[pl.ds((d * ill_n + peer) * (liq_n * plane_rows), liq_n * plane_rows)],
            dst_ref=terms_in.at[slot], send_sem=terms_send.at[slot], recv_sem=terms_recv.at[slot],
            device_id={"ill": peer}, device_id_type=MESH_ID,
        )

    def owner_copy(d, step):
        peer = peer_of(liq_me, step, liq_n)
        slot = d * (liq_n - 1) + step - 1
        return pltpu.make_async_remote_copy(
            src_ref=owner_sum.at[d * liq_n + peer], dst_ref=owner_in.at[slot],
            send_sem=owner_send.at[slot], recv_sem=owner_recv.at[slot],
            device_id={"liq": peer}, device_id_type=MESH_ID,
        )

    loads[2].wait()
    value_copy(0, value_ref).start()
    drifted = dot(first_mat[...], value_ref[...])
    value_copy(0, value_ref).wait_recv()
    drifted = drifted + dot(first_up[...], near_value[0])
    pencil[liq_me] = lax.rsqrt(drifted)
    for half in range(2):
        for step in far_first:
            pencil_copy(0, half, step).start()

    wide = constant * dot(dot(spread, transition), spread_t)
    second_mat[...] = wide * local
    second_up[...] = wide * upper

    first_d = as_float(dur_me == 0)
    stay = [keep_ref[d] for d in range(durables)]
    stay[0] = first_d + (1.0 - first_d) * stay[0]
    back_d, back_rest = split_by(iota((rows, rows), 1), plane_rows)
    back_a = split_by(back_rest, ill_rows)[1]
    stays = jnp.zeros((rows, rows), jnp.float32)
    for d in range(durables):
        stays = jnp.where(back_d == d, stay[d], stays)
    mix = jnp.where(back_d == row_d, stays, 0.0) + jnp.where(back_d == row_d + 1, 1.0 - stays, 0.0)
    mix = jnp.where(back_a == row_a, mix, 0.0)
    back_z = split_by(split_by(iota((incomes, rows), 1), plane_rows)[1], ill_rows)[0]
    turned = lax.dot_general(spread, transition, NT, precision=HIGHEST_PREC, preferred_element_type=jnp.float32)
    wide = dot(turned, as_float(iota((incomes, rows), 0) == back_z))
    next_mat[...] = wide * mix
    in_z, in_a = split_by(iota((incomes, plane_rows), 1), ill_rows)
    wide = dot(turned, as_float(iota((incomes, plane_rows), 0) == in_z))
    in_row = split_by(iota((rows, plane_rows), 0), group)[1]
    in_row_d, in_row_a = split_by(in_row, ill_rows)
    in_col_a = split_by(iota((rows, plane_rows), 1), ill_rows)[1]
    next_in[...] = jnp.where((in_row_d == durables - 1) & (in_row_a == in_col_a), wide, 0.0)

    def block_of(position):
        block = jnp.zeros(position.shape, jnp.int32)
        for h in range(1, liq_n):
            block = block + jnp.where(position >= h * liq_rows, 1, 0)
        return block, position - block * liq_rows

    for load in loads[3:]:
        load.wait()
    target_hi[...], target_lo[...] = block_of(target_ref[...])

    def interpolate(k, tile):
        span = pl.ds(tile * TILE, TILE)
        index = index_ref[span, :]
        low_block, low_lane = block_of(index)
        high_block, high_lane = block_of(index + 1)
        low = high = None
        for h in range(liq_n):
            block = pencil[k * liq_n + h, span, :]
            low_h = jnp.take_along_axis(block, low_lane, axis=1, mode="promise_in_bounds")
            high_h = jnp.take_along_axis(block, high_lane, axis=1, mode="promise_in_bounds")
            low = low_h if h == 0 else jnp.where(low_block == h, low_h, low)
            high = high_h if h == 0 else jnp.where(high_block == h, high_h, high)
        weight = weight_ref[span, :]
        return weight * low + (1.0 - weight) * high

    tiles = rows // TILE
    halves = (range(tiles // 2), range(tiles // 2, tiles))

    def first_policy(half):
        for step in far_first:
            pencil_copy(0, half, step).wait_recv()
        for tile in halves[half]:
            span = pl.ds(tile * TILE, TILE)
            chosen = interpolate(0, tile)
            value_two[span, :] = GROSS_RATE / (chosen * chosen)
            share = jnp.clip(lottery_ref[span, :] + SLOPE_GAIN * (chosen - steady_ref[span, :]), 0.0, 1.0)
            mass = population_ref[span, :]
            mass_low[span, :] = mass * share
            mass_high[span, :] = mass * (1.0 - share)

    lanes = 2 * liq_n
    sub = iota((lanes, liq_rows), 0)
    lane = iota((lanes, liq_rows), 1)
    sub_block = jnp.where(sub < liq_n, sub, sub - liq_n)
    lane_row = iota((liq_rows, liq_rows), 0)
    per_tile = TILE // group

    def scatter_tile(d, tile):
        span = pl.ds(pl.multiple_of(tile * TILE, TILE), TILE)
        low_t, high_t, hi_t, lo_t = mass_low[span, :], mass_high[span, :], target_hi[span, :], target_lo[span, :]
        for zz in range(per_tile):
            z = tile * per_tile + zz
            totals = []
            for a in range(ill_rows):
                k = zz * group + d * ill_rows + a
                both = jnp.where(sub < liq_n, low_t[k : k + 1, :], high_t[k : k + 1, :])
                both = jnp.where(hi_t[k : k + 1, :] == sub_block, both, 0.0)
                rounded = both.astype(jnp.bfloat16).astype(jnp.float32)
                parts = jnp.concatenate([both, both - rounded], axis=0).astype(jnp.bfloat16)
                hot = as_float(lane_row == lo_t[k : k + 1, :]).astype(jnp.bfloat16)
                placed = lax.dot_general(parts, hot, NT, preferred_element_type=jnp.float32)
                placed = placed[:lanes] + placed[lanes:]
                moved = pltpu.roll(placed, 1, 1)
                same = pltpu.roll(moved, liq_n, 0)
                prior = pltpu.roll(moved, liq_n + 1, 0)
                totals.append(placed + jnp.where(lane > 0, same, jnp.where(sub > 0, prior, 0.0)))
            for dest in range(ill_n * ill_rows):
                out = None
                for a in range(ill_rows):
                    here = as_float(ill_target_ref[d * ill_rows + a, z] == dest) * totals[a]
                    out = here if out is None else out + here
                base = (d * ill_n + dest // ill_rows) * liq_n * plane_rows + z * ill_rows + dest % ill_rows
                terms[pl.ds(base, liq_n, stride=plane_rows), :] = out[:liq_n]

    def scatter(d, half):
        def step(pair, carry):
            scatter_tile(d, halves[half].start + 2 * pair)
            scatter_tile(d, halves[half].start + 2 * pair + 1)
            return carry

        lax.fori_loop(0, tiles // 4, step, 0)

    def send_owners(d):
        for step in range(1, ill_n):
            terms_copy(d, step).wait_recv()
        for h in range(liq_n):
            start = pl.multiple_of(((d * ill_n + ill_me) * liq_n + h) * plane_rows, TILE)
            total = terms[pl.ds(start, plane_rows), :]
            for step in range(1, ill_n):
                total = total + terms_in[d * (ill_n - 1) + step - 1, pl.ds(h * plane_rows, plane_rows), :]
            owner_sum[d * liq_n + h] = total
        for step in far_first:
            owner_copy(d, step).start()

    def collect(d):
        for step in far_first:
            owner_copy(d, step).wait_recv()
        total = owner_sum[d * liq_n + liq_me]
        for step in range(1, liq_n):
            total = total + owner_in[d * (liq_n - 1) + step - 1]
        settled[pl.ds(d * plane_rows, plane_rows), :] = total
        return total

    def second_policy(half):
        for step in far_first:
            pencil_copy(1, half, step).wait_recv()
        for tile in halves[half]:
            consumption_ref[pl.ds(tile * TILE, TILE), :] = interpolate(1, tile)

    first_policy(0)
    scatter(0, 0)
    first_policy(1)
    value_copy(1, value_two).start()
    scatter(0, 1)
    for step in range(1, ill_n):
        terms_copy(0, step).start()
    value_copy(1, value_two).wait_recv()
    drifted = dot(second_mat[...], value_two[...]) + dot(second_up[...], near_value[1])
    pencil[liq_n + liq_me] = lax.rsqrt(drifted)
    for step in far_first:
        pencil_copy(1, 0, step).start()
    for d in range(1, durables):
        scatter(d, 0)
        if d == 1:
            send_owners(0)
        scatter(d, 1)
        for step in range(1, ill_n):
            terms_copy(d, step).start()
    for d in range(1, durables):
        send_owners(d)
    for step in far_first:
        pencil_copy(1, 1, step).start()

    depart_copy = pltpu.make_async_remote_copy(
        src_ref=depart, dst_ref=depart_in, send_sem=depart_send.at[0], recv_sem=depart_recv.at[0],
        device_id={"dur": jnp.maximum(dur_me - 1, 0)}, device_id_type=MESH_ID,
    )

    second_policy(0)
    depart[...] = (1.0 - stay[0]) * collect(0)

    @pl.when(dur_me > 0)
    def _():
        depart_copy.start()

    for d in range(1, durables):
        collect(d)
    next_ref[...] = dot(next_mat[...], settled[...])
    second_policy(1)
    stores = [
        pltpu.make_async_copy(consumption_ref, consumption_hbm, store_sem.at[0]),
        pltpu.make_async_copy(next_ref, next_hbm, store_sem.at[1]),
    ]
    stores[0].start()

    @pl.when(dur_me < dur_n - 1)
    def _():
        depart_copy.wait_recv()
        next_ref[...] += dot(next_in[...], depart_in[...])

    stores[1].start()

    value_copy(0, value_ref).wait_send()
    value_copy(1, value_two).wait_send()
    for step in range(1, liq_n):
        for k in range(2):
            for half in range(2):
                pencil_copy(k, half, step).wait_send()
        for d in range(durables):
            owner_copy(d, step).wait_send()
    for step in range(1, ill_n):
        for d in range(durables):
            terms_copy(d, step).wait_send()

    @pl.when(dur_me > 0)
    def _():
        depart_copy.wait_send()

    stores[0].wait()
    stores[1].wait()


def body(
    marginal_value,
    transition,
    discount_shock,
    illiquid_drift,
    durable_keep,
    bracket_index,
    bracket_weight,
    steady_consumption,
    lottery_weight,
    liquid_target,
    illiquid_target,
    population,
):
    shape = marginal_value.shape
    incomes, durables, ill_rows, liq_rows = shape
    liq_n, ill_n, dur_n = (lax.axis_size(name) for name in ("liq", "ill", "dur"))
    rows = incomes * durables * ill_rows
    plane_rows = incomes * ill_rows
    flat = lambda x: x.reshape(rows, liq_rows)
    anywhere = pl.BlockSpec(memory_space=pl.ANY)
    smem = pl.BlockSpec(memory_space=pltpu.SMEM)
    f32 = jnp.float32
    block = (rows, liq_rows)
    dma = pltpu.SemaphoreType.DMA
    result = jax.ShapeDtypeStruct(block, f32)
    dims = (incomes, durables, ill_rows, liq_rows, liq_n, ill_n, dur_n)
    outs = pl.pallas_call(
        functools.partial(kernel, dims),
        out_shape=(result, result),
        in_specs=[anywhere, anywhere, anywhere, smem, smem] + [anywhere] * 5 + [smem, anywhere],
        out_specs=(anywhere, anywhere),
        scratch_shapes=[
            pltpu.VMEM(block, f32),
            pltpu.VMEM((incomes, incomes), f32),
            pltpu.VMEM((1, incomes), f32),
            pltpu.VMEM(block, jnp.int32),
            pltpu.VMEM(block, f32),
            pltpu.VMEM(block, f32),
            pltpu.VMEM(block, f32),
            pltpu.VMEM(block, jnp.int32),
            pltpu.VMEM(block, f32),
            pltpu.VMEM(block, f32),
            pltpu.VMEM(block, f32),
            dma((9,)),
            dma((2,)),
            pltpu.VMEM((rows, rows), f32),
            pltpu.VMEM((rows, rows), f32),
            pltpu.VMEM((rows, rows), f32),
            pltpu.VMEM((rows, rows), f32),
            pltpu.VMEM((rows, rows), f32),
            pltpu.VMEM((rows, plane_rows), f32),
            pltpu.VMEM((2,) + block, f32),
            pltpu.VMEM(block, f32),
            pltpu.VMEM((2 * liq_n,) + block, f32),
            pltpu.VMEM(block, f32),
            pltpu.VMEM(block, f32),
            pltpu.VMEM(block, jnp.int32),
            pltpu.VMEM(block, jnp.int32),
            pltpu.VMEM((ill_n * liq_n * rows, liq_rows), f32),
            pltpu.VMEM((durables * (ill_n - 1), liq_n * plane_rows, liq_rows), f32),
            pltpu.VMEM((durables * liq_n, plane_rows, liq_rows), f32),
            pltpu.VMEM((durables * (liq_n - 1), plane_rows, liq_rows), f32),
            pltpu.VMEM(block, f32),
            pltpu.VMEM((plane_rows, liq_rows), f32),
            pltpu.VMEM((plane_rows, liq_rows), f32),
            dma((2,)),
            dma((2,)),
            dma((4 * liq_n,)),
            dma((4 * liq_n,)),
            dma((durables * (ill_n - 1),)),
            dma((durables * (ill_n - 1),)),
            dma((durables * (liq_n - 1),)),
            dma((durables * (liq_n - 1),)),
            dma((1,)),
            dma((1,)),
        ],
        compiler_params=pltpu.CompilerParams(collective_id=0, has_side_effects=True),
        name="window",
    )(
        flat(marginal_value),
        transition,
        discount_shock.reshape(1, incomes),
        illiquid_drift,
        durable_keep,
        flat(bracket_index),
        flat(bracket_weight),
        flat(steady_consumption),
        flat(lottery_weight),
        flat(liquid_target),
        jnp.transpose(illiquid_target, (1, 2, 0)).reshape(durables * ill_rows, incomes),
        flat(population),
    )
    return tuple(out.reshape(shape) for out in outs)


def solution(mesh):
    in_specs = (
        P(None, "dur", "ill", "liq"),
        P(),
        P(),
        P("ill"),
        P("dur"),
        P(None, "dur", "ill", "liq"),
        P(None, "dur", "ill", "liq"),
        P(None, "dur", "ill", "liq"),
        P(None, "dur", "ill", "liq"),
        P(None, "dur", "ill", "liq"),
        P(None, "dur", "ill"),
        P(None, "dur", "ill", "liq"),
    )
    out_specs = (P(None, "dur", "ill", "liq"), P(None, "dur", "ill", "liq"))
    return jax.shard_map(body, mesh=mesh, in_specs=in_specs, out_specs=out_specs, check_vma=False)
```

time: 31.3 us -> 26.4 us (0.84)
  Pallas kernels: 28.3 us -> 23.3 us
    pallas_call x1, Pallas kernels: 28.3 us -> 23.3 us  [body(): pl.pallas_call(functools.partial(kernel, dims), out_shape=(result, result...]
where the time goes in v2:
time: 26.4 us; the launch traced here: 26.1 us
  Pallas kernels  23.3 us (88%)
  local copies, waits for them, and re-layouts  2.14 us (8%)
  between operations  0.65 us (2%)
    pallas_call x1, Pallas kernels, body(): pl.pallas_call(functools.partial(kernel, dims), out_shape=(result, result...  23.3 us
    unnamed x4, local copies, waits for them, and re-layouts  2.14 us

profile of v2, /device:TPU:0, one launch (start us, length us, event | category | flops | bytes accessed | tf_op | source)
XLA Modules:
  0.0 26.1 jit_solution(15992114398756859540)
XLA Ops:
  0.6 23.3 %window.1 = (f32[128,128]{1,0:T(8,128)}, f32[128,128]{1,0:T(8,128)}) custom-call(f32[128,128]{1,0:T(8,128)} %bitcast.15, f32[32,32]{1,0:T(8,128)} %transition_hbm.1, f32[1,32]{1,0:T(1,128)} %bitcast.23, f32[2]{0:T(128)} %drift_ref.1, f32[2]{0:T(128)} %keep_ref.1, s32[128,128]{1,0:T(8,128)} %bitcast.16, f32[128,128]{1,0:T(8,128)} %bitcast.17, ...), custom_call_target="tpu_custom_call" | custom-call | tf_op jit(solution)/shard_map/window/pallas_call | solution.py:401
  23.9 0.0 copy-start
  24.0 1.5 %copy.16 = f32[32,2,2,128]{3,2,1,0:T(2,128)} copy(f32[32,2,2,128]{3,2,1,0:T(2,128)} %bitcast.14) | data formatting | bytes 131072
  25.5 0.0 copy-done
  25.5 0.6 %copy.17 = f32[32,2,2,128]{3,2,1,0:T(2,128)} copy(f32[32,2,2,128]{3,2,1,0:T(2,128)S(1)} %bitcast.13) | data formatting | bytes 131072
Async XLA Ops:
  23.9 1.5 %copy-start = (f32[128,128]{1,0:T(8,128)S(1)}, f32[128,128]{1,0:T(8,128)}, u32[]{:S(2)}) copy-start(f32[128,128]{1,0:T(8,128)} %get-tuple-element.5) | copy-start | bytes 196612

commit v3 on v2

--- a/solution.py
+++ b/solution.py
@@ -48,9 +48,9 @@
     dims,
     value_hbm, transition_hbm, shock_hbm, drift_ref, keep_ref, index_hbm, weight_hbm,
     steady_hbm, lottery_hbm, target_hbm, ill_target_ref, population_hbm,
-    consumption_hbm, next_hbm,
+    consumption_ref, next_ref,
     value_ref, transition_ref, shock_ref, index_ref, weight_ref, steady_ref, lottery_ref, target_ref,
-    population_ref, consumption_ref, next_ref, load_sem, store_sem,
+    population_ref, load_sem,
     first_mat, first_up, second_mat, second_up, next_mat, next_in,
     near_value, value_two, pencil, mass_low, mass_high, target_hi, target_lo,
     terms, terms_in, owner_sum, owner_in, settled, depart, depart_in,
@@ -338,18 +338,11 @@
         collect(d)
     next_ref[...] = dot(next_mat[...], settled[...])
     second_policy(1)
-    stores = [
-        pltpu.make_async_copy(consumption_ref, consumption_hbm, store_sem.at[0]),
-        pltpu.make_async_copy(next_ref, next_hbm, store_sem.at[1]),
-    ]
-    stores[0].start()
 
     @pl.when(dur_me < dur_n - 1)
     def _():
         depart_copy.wait_recv()
         next_ref[...] += dot(next_in[...], depart_in[...])
-
-    stores[1].start()
 
     value_copy(0, value_ref).wait_send()
     value_copy(1, value_two).wait_send()
@@ -367,8 +360,16 @@
     def _():
         depart_copy.wait_send()
 
-    stores[0].wait()
-    stores[1].wait()
+
+def store(consumption_ref, next_ref, consumption_hbm, next_hbm, sem):
+    copies = [
+        pltpu.make_async_copy(consumption_ref, consumption_hbm, sem.at[0]),
+        pltpu.make_async_copy(next_ref, next_hbm, sem.at[1]),
+    ]
+    for copy in copies:
+        copy.start()
+    for copy in copies:
+        copy.wait()
 
 
 def body(
@@ -396,13 +397,15 @@
     f32 = jnp.float32
     block = (rows, liq_rows)
     dma = pltpu.SemaphoreType.DMA
+    vmem = pl.BlockSpec(memory_space=pltpu.VMEM)
+    held = pltpu.VMEM(block, f32)
     result = jax.ShapeDtypeStruct(block, f32)
     dims = (incomes, durables, ill_rows, liq_rows, liq_n, ill_n, dur_n)
     outs = pl.pallas_call(
         functools.partial(kernel, dims),
-        out_shape=(result, result),
+        out_shape=(held, held),
         in_specs=[anywhere, anywhere, anywhere, smem, smem] + [anywhere] * 5 + [smem, anywhere],
-        out_specs=(anywhere, anywhere),
+        out_specs=(vmem, vmem),
         scratch_shapes=[
             pltpu.VMEM(block, f32),
             pltpu.VMEM((incomes, incomes), f32),
@@ -413,10 +416,7 @@
             pltpu.VMEM(block, f32),
             pltpu.VMEM(block, jnp.int32),
             pltpu.VMEM(block, f32),
-            pltpu.VMEM(block, f32),
-            pltpu.VMEM(block, f32),
             dma((9,)),
-            dma((2,)),
             pltpu.VMEM((rows, rows), f32),
             pltpu.VMEM((rows, rows), f32),
             pltpu.VMEM((rows, rows), f32),
@@ -464,6 +464,14 @@
         jnp.transpose(illiquid_target, (1, 2, 0)).reshape(durables * ill_rows, incomes),
         flat(population),
     )
+    outs = pl.pallas_call(
+        store,
+        out_shape=(result, result),
+        in_specs=[vmem, vmem],
+        out_specs=(anywhere, anywhere),
+        scratch_shapes=[dma((2,))],
+        name="store",
+    )(*(pltpu.with_memory_space_constraint(out, pltpu.VMEM) for out in outs))
     return tuple(out.reshape(shape) for out in outs)
 
 

time: 26.4 us -> 24.3 us (0.920)
  local copies, waits for them, and re-layouts: 2.14 us -> 0 us
    unnamed x4 -> x0, local copies, waits for them, and re-layouts: 2.14 us -> none
    pallas_call x1 -> x2, Pallas kernels: 23.3 us -> 23.4 us  [the longest x1 22.7 us: body(): pl.pallas_call(functools.partial(kernel, dims), out_shape=(held, held), i...]
where the time goes in v3:
time: 24.3 us; the launch traced here: 24 us
  Pallas kernels  23.4 us (96%)
  between operations  0.64 us (3%)
    pallas_call x1, Pallas kernels, body(): pl.pallas_call(functools.partial(kernel, dims), out_shape=(held, held), i...  22.7 us
    pallas_call x1, Pallas kernels, body(): pl.pallas_call(store, out_shape=(result, result), in_specs=[vmem, vmem],...  0.67 us

profile of v3, /device:TPU:0, one launch (start us, length us, event | category | flops | bytes accessed | tf_op | source)
XLA Modules:
  0.0 24.0 jit_solution(11897806355921373363)
XLA Ops:
  0.6 22.7 %window.1 = (f32[128,128]{1,0:T(8,128)S(1)}, f32[128,128]{1,0:T(8,128)S(1)}) custom-call(f32[128,128]{1,0:T(8,128)} %bitcast.13, f32[32,32]{1,0:T(8,128)} %transition_hbm.1, f32[1,32]{1,0:T(1,128)} %bitcast.21, f32[2]{0:T(128)} %drift_ref.1, f32[2]{0:T(128)} %keep_ref.1, s32[128,128]{1,0:T(8,128)} %bitcast.14, f32[128,128]{1,0:T(8,128)} %bitcast.15, ...), custom_call_target="tpu_custom_call" | custom-call | tf_op jit(solution)/shard_map/window/pallas_call | solution.py:404
  23.4 0.7 %store.1 = (f32[128,128]{1,0:T(8,128)}, f32[128,128]{1,0:T(8,128)}) custom-call(f32[128,128]{1,0:T(8,128)S(1)} %get-tuple-element.6.consumption_ref, f32[128,128]{1,0:T(8,128)S(1)} %get-tuple-element.7.next_ref), custom_call_target="tpu_custom_call" | custom-call | tf_op jit(solution)/shard_map/store/pallas_call | solution.py:467

commit v4 on v3

--- a/solution.py
+++ b/solution.py
@@ -46,14 +46,14 @@
 
 def kernel(
     dims,
-    value_hbm, transition_hbm, shock_hbm, drift_ref, keep_ref, index_hbm, weight_hbm,
-    steady_hbm, lottery_hbm, target_hbm, ill_target_ref, population_hbm,
+    value_hbm, transition_hbm, shock_hbm, drift_hbm, keep_hbm, index_hbm, weight_hbm,
+    steady_hbm, lottery_hbm, target_hbm, ill_target_hbm, population_hbm,
     consumption_ref, next_ref,
     value_ref, transition_ref, shock_ref, index_ref, weight_ref, steady_ref, lottery_ref, target_ref,
-    population_ref, load_sem,
+    population_ref, drift_ref, keep_ref, ill_target_ref, load_sem,
     first_mat, first_up, second_mat, second_up, next_mat, next_in,
     near_value, value_two, pencil, mass_low, mass_high, target_hi, target_lo,
-    terms, terms_in, owner_sum, owner_in, settled, depart, depart_in,
+    placed_rows, terms, terms_in, owner_sum, owner_in, settled, depart, depart_in,
     value_send, value_recv, pencil_send, pencil_recv, terms_send, terms_recv,
     owner_send, owner_recv, depart_send, depart_recv,
 ):
@@ -82,15 +82,16 @@
     loads = [
         pltpu.make_async_copy(source, held, load_sem.at[slot])
         for slot, (source, held) in enumerate((
-            (transition_hbm, transition_ref), (shock_hbm, shock_ref), (value_hbm, value_ref),
+            (transition_hbm, transition_ref), (shock_hbm, shock_ref), (drift_hbm, drift_ref), (value_hbm, value_ref),
+            (keep_hbm, keep_ref), (ill_target_hbm, ill_target_ref),
             (index_hbm, index_ref), (weight_hbm, weight_ref), (target_hbm, target_ref),
             (lottery_hbm, lottery_ref), (steady_hbm, steady_ref), (population_hbm, population_ref),
         ))
     ]
     for load in loads:
         load.start()
-    loads[0].wait()
-    loads[1].wait()
+    for load in loads[:3]:
+        load.wait()
 
     transition = transition_ref[...]
     row_z, row_rest = split_by(iota((rows, rows), 0), group)
@@ -136,6 +137,21 @@
             device_id={"liq": peer_of(liq_me, step, liq_n)}, device_id_type=MESH_ID,
         )
 
+    def pencil_relay(half):
+        near, far = (1, 2) if half == 0 else (2, 1)
+        slot = (2 + half) * liq_n
+        part = pencil.at[liq_n + peer_of(liq_me, near, liq_n), pl.ds(half * half_rows, half_rows)]
+        return pltpu.make_async_remote_copy(
+            src_ref=part, dst_ref=part, send_sem=pencil_send.at[slot], recv_sem=pencil_recv.at[slot],
+            device_id={"liq": peer_of(liq_me, far, liq_n)}, device_id_type=MESH_ID,
+        )
+
+    relayed = liq_n == 4
+    if relayed:
+        early, late = [(0, 1), (1, 2)], [(1, 1), (0, 2)]
+    else:
+        early, late = [(0, step) for step in far_first], [(1, step) for step in far_first]
+
     def terms_copy(d, step):
         peer = peer_of(ill_me, step, ill_n)
         slot = d * (ill_n - 1) + step - 1
@@ -154,7 +170,7 @@
             device_id={"liq": peer}, device_id_type=MESH_ID,
         )
 
-    loads[2].wait()
+    loads[3].wait()
     value_copy(0, value_ref).start()
     drifted = dot(first_mat[...], value_ref[...])
     value_copy(0, value_ref).wait_recv()
@@ -167,6 +183,9 @@
     wide = constant * dot(dot(spread, transition), spread_t)
     second_mat[...] = wide * local
     second_up[...] = wide * upper
+
+    for load in loads[4:]:
+        load.wait()
 
     first_d = as_float(dur_me == 0)
     stay = [keep_ref[d] for d in range(durables)]
@@ -195,9 +214,8 @@
             block = block + jnp.where(position >= h * liq_rows, 1, 0)
         return block, position - block * liq_rows
 
-    for load in loads[3:]:
-        load.wait()
-    target_hi[...], target_lo[...] = block_of(target_ref[...])
+    target_hi[...], lo = block_of(target_ref[...])
+    target_lo[...] = lo.astype(jnp.float32)
 
     def interpolate(k, tile):
         span = pl.ds(tile * TILE, TILE)
@@ -231,9 +249,11 @@
 
     lanes = 2 * liq_n
     sub = iota((lanes, liq_rows), 0)
-    lane = iota((lanes, liq_rows), 1)
+    lane_at = iota((TILE, liq_rows), 1)
     sub_block = jnp.where(sub < liq_n, sub, sub - liq_n)
-    lane_row = iota((liq_rows, liq_rows), 0)
+    lane_row = iota((liq_rows, liq_rows), 0).astype(jnp.float32).astype(jnp.bfloat16)
+    one = jnp.ones((liq_rows, liq_rows), jnp.bfloat16)
+    nil = jnp.zeros((liq_rows, liq_rows), jnp.bfloat16)
     per_tile = TILE // group
 
     def scatter_tile(d, tile):
@@ -248,28 +268,44 @@
                 both = jnp.where(hi_t[k : k + 1, :] == sub_block, both, 0.0)
                 rounded = both.astype(jnp.bfloat16).astype(jnp.float32)
                 parts = jnp.concatenate([both, both - rounded], axis=0).astype(jnp.bfloat16)
-                hot = as_float(lane_row == lo_t[k : k + 1, :]).astype(jnp.bfloat16)
+                place = jnp.broadcast_to(lo_t[k : k + 1, :], (2 * TILE, liq_rows)).astype(jnp.bfloat16)
+                place = jnp.concatenate([place] * (liq_rows // (2 * TILE)), axis=0)
+                hot = jnp.where(lane_row == place, one, nil)
                 placed = lax.dot_general(parts, hot, NT, preferred_element_type=jnp.float32)
                 placed = placed[:lanes] + placed[lanes:]
-                moved = pltpu.roll(placed, 1, 1)
-                same = pltpu.roll(moved, liq_n, 0)
-                prior = pltpu.roll(moved, liq_n + 1, 0)
-                totals.append(placed + jnp.where(lane > 0, same, jnp.where(sub > 0, prior, 0.0)))
+                totals.append(placed)
             for dest in range(ill_n * ill_rows):
                 out = None
                 for a in range(ill_rows):
                     here = as_float(ill_target_ref[d * ill_rows + a, z] == dest) * totals[a]
                     out = here if out is None else out + here
-                base = (d * ill_n + dest // ill_rows) * liq_n * plane_rows + z * ill_rows + dest % ill_rows
-                terms[pl.ds(base, liq_n, stride=plane_rows), :] = out[:liq_n]
+                base = dest // ill_rows * lanes * plane_rows + z * ill_rows + dest % ill_rows
+                placed_rows[pl.ds(base, lanes, stride=plane_rows), :] = out
+
+    unroll = tiles // 2
 
     def scatter(d, half):
         def step(pair, carry):
-            scatter_tile(d, halves[half].start + 2 * pair)
-            scatter_tile(d, halves[half].start + 2 * pair + 1)
+            for turn in range(unroll):
+                scatter_tile(d, halves[half].start + unroll * pair + turn)
             return carry
 
-        lax.fori_loop(0, tiles // 4, step, 0)
+        lax.fori_loop(0, tiles // 2 // unroll, step, 0)
+
+    def send_terms(d):
+        for owner in range(ill_n):
+            for piece in range(plane_rows // TILE):
+                carried = None
+                for h in range(liq_n):
+                    low_at = (owner * lanes + h) * plane_rows + piece * TILE
+                    low = placed_rows[pl.ds(low_at, TILE), :]
+                    moved = pltpu.roll(placed_rows[pl.ds(low_at + liq_n * plane_rows, TILE), :], 1, 1)
+                    edge = jnp.where(lane_at > 0, moved, 0.0 if carried is None else carried)
+                    carried = moved
+                    out_at = ((d * ill_n + owner) * liq_n + h) * plane_rows + piece * TILE
+                    terms[pl.ds(out_at, TILE), :] = low + edge
+        for step in range(1, ill_n):
+            terms_copy(d, step).start()
 
     def send_owners(d):
         for step in range(1, ill_n):
@@ -292,10 +328,16 @@
         settled[pl.ds(d * plane_rows, plane_rows), :] = total
         return total
 
-    def second_policy(half):
-        for step in far_first:
+    def second_policy():
+        if relayed:
+            for half in range(2):
+                pencil_relay(half).wait_recv()
+        else:
+            for half, step in early:
+                pencil_copy(1, half, step).wait_recv()
+        for half, step in late:
             pencil_copy(1, half, step).wait_recv()
-        for tile in halves[half]:
+        for tile in range(tiles):
             consumption_ref[pl.ds(tile * TILE, TILE), :] = interpolate(1, tile)
 
     first_policy(0)
@@ -303,31 +345,33 @@
     first_policy(1)
     value_copy(1, value_two).start()
     scatter(0, 1)
-    for step in range(1, ill_n):
-        terms_copy(0, step).start()
+    send_terms(0)
     value_copy(1, value_two).wait_recv()
     drifted = dot(second_mat[...], value_two[...]) + dot(second_up[...], near_value[1])
     pencil[liq_n + liq_me] = lax.rsqrt(drifted)
-    for step in far_first:
-        pencil_copy(1, 0, step).start()
+    for half, step in early:
+        pencil_copy(1, half, step).start()
     for d in range(1, durables):
         scatter(d, 0)
         if d == 1:
             send_owners(0)
+            for half, step in late:
+                pencil_copy(1, half, step).start()
         scatter(d, 1)
-        for step in range(1, ill_n):
-            terms_copy(d, step).start()
+        send_terms(d)
     for d in range(1, durables):
         send_owners(d)
-    for step in far_first:
-        pencil_copy(1, 1, step).start()
+    if relayed:
+        for half, step in early:
+            pencil_copy(1, half, step).wait_recv()
+        for half in range(2):
+            pencil_relay(half).start()
 
     depart_copy = pltpu.make_async_remote_copy(
         src_ref=depart, dst_ref=depart_in, send_sem=depart_send.at[0], recv_sem=depart_recv.at[0],
         device_id={"dur": jnp.maximum(dur_me - 1, 0)}, device_id_type=MESH_ID,
     )
 
-    second_policy(0)
     depart[...] = (1.0 - stay[0]) * collect(0)
 
     @pl.when(dur_me > 0)
@@ -337,7 +381,7 @@
     for d in range(1, durables):
         collect(d)
     next_ref[...] = dot(next_mat[...], settled[...])
-    second_policy(1)
+    second_policy()
 
     @pl.when(dur_me < dur_n - 1)
     def _():
@@ -347,11 +391,15 @@
     value_copy(0, value_ref).wait_send()
     value_copy(1, value_two).wait_send()
     for step in range(1, liq_n):
-        for k in range(2):
-            for half in range(2):
-                pencil_copy(k, half, step).wait_send()
+        for half in range(2):
+            pencil_copy(0, half, step).wait_send()
         for d in range(durables):
             owner_copy(d, step).wait_send()
+    for half, step in early + late:
+        pencil_copy(1, half, step).wait_send()
+    if relayed:
+        for half in range(2):
+            pencil_relay(half).wait_send()
     for step in range(1, ill_n):
         for d in range(durables):
             terms_copy(d, step).wait_send()
@@ -393,7 +441,6 @@
     plane_rows = incomes * ill_rows
     flat = lambda x: x.reshape(rows, liq_rows)
     anywhere = pl.BlockSpec(memory_space=pl.ANY)
-    smem = pl.BlockSpec(memory_space=pltpu.SMEM)
     f32 = jnp.float32
     block = (rows, liq_rows)
     dma = pltpu.SemaphoreType.DMA
@@ -404,7 +451,7 @@
     outs = pl.pallas_call(
         functools.partial(kernel, dims),
         out_shape=(held, held),
-        in_specs=[anywhere, anywhere, anywhere, smem, smem] + [anywhere] * 5 + [smem, anywhere],
+        in_specs=[anywhere] * 12,
         out_specs=(vmem, vmem),
         scratch_shapes=[
             pltpu.VMEM(block, f32),
@@ -416,7 +463,10 @@
             pltpu.VMEM(block, f32),
             pltpu.VMEM(block, jnp.int32),
             pltpu.VMEM(block, f32),
-            dma((9,)),
+            pltpu.SMEM((ill_rows,), f32),
+            pltpu.SMEM((durables,), f32),
+            pltpu.SMEM((durables * ill_rows, incomes), jnp.int32),
+            dma((12,)),
             pltpu.VMEM((rows, rows), f32),
             pltpu.VMEM((rows, rows), f32),
             pltpu.VMEM((rows, rows), f32),
@@ -429,7 +479,8 @@
             pltpu.VMEM(block, f32),
             pltpu.VMEM(block, f32),
             pltpu.VMEM(block, jnp.int32),
-            pltpu.VMEM(block, jnp.int32),
+            pltpu.VMEM(block, f32),
+            pltpu.VMEM((2 * ill_n * liq_n * plane_rows, liq_rows), f32),
             pltpu.VMEM((ill_n * liq_n * rows, liq_rows), f32),
             pltpu.VMEM((durables * (ill_n - 1), liq_n * plane_rows, liq_rows), f32),
             pltpu.VMEM((durables * liq_n, plane_rows, liq_rows), f32),

time: 24.3 us -> 22.1 us (0.909)
  Pallas kernels: 23.4 us -> 21.2 us
    pallas_call x1, Pallas kernels: 22.7 us -> 20.5 us  [body(): pl.pallas_call(functools.partial(kernel, dims), out_shape=(held, held), i...]
where the time goes in v4:
time: 22.1 us; the launch traced here: 21.8 us
  Pallas kernels  21.2 us (96%)
  between operations  0.64 us (3%)
    pallas_call x1, Pallas kernels, body(): pl.pallas_call(functools.partial(kernel, dims), out_shape=(held, held), i...  20.5 us
    pallas_call x1, Pallas kernels, body(): pl.pallas_call(store, out_shape=(result, result), in_specs=[vmem, vmem],...  0.67 us

profile of v4, /device:TPU:0, one launch (start us, length us, event | category | flops | bytes accessed | tf_op | source)
XLA Modules:
  0.0 21.8 jit_solution(6120246534239686594)
XLA Ops:
  0.6 20.5 %window.1 = (f32[128,128]{1,0:T(8,128)S(1)}, f32[128,128]{1,0:T(8,128)S(1)}) custom-call(f32[128,128]{1,0:T(8,128)} %bitcast.13, f32[32,32]{1,0:T(8,128)} %transition_hbm.1, f32[1,32]{1,0:T(1,128)} %bitcast.21, f32[2]{0:T(128)} %drift_hbm.1, f32[2]{0:T(128)} %keep_hbm.1, s32[128,128]{1,0:T(8,128)} %bitcast.14, f32[128,128]{1,0:T(8,128)} %bitcast.15, ...), custom_call_target="tpu_custom_call" | custom-call | tf_op jit(solution)/shard_map/window/pallas_call | solution.py:451
  21.2 0.7 %store.1 = (f32[128,128]{1,0:T(8,128)}, f32[128,128]{1,0:T(8,128)}) custom-call(f32[128,128]{1,0:T(8,128)S(1)} %get-tuple-element.6.consumption_ref, f32[128,128]{1,0:T(8,128)S(1)} %get-tuple-element.7.next_ref), custom_call_target="tpu_custom_call" | custom-call | tf_op jit(solution)/shard_map/store/pallas_call | solution.py:518
